TPU v7x, 256 devices: a whole 4x4x8 slice. The times are simulated.
256 devices in a mesh: cable: 4 (over y), fx: 32 (over z, x), fz: 2 (over core).
Axes of the slice: x: 4, y: 4, z: 8, core: 2. Of those that a mesh axis runs over, the one named last changes fastest.
Arguments:
- velocity: float32 [3, 256, 64, 256], P(None, 'fx', 'cable', 'fz'), may hold values from -6 to 6
- viscosity: float32 [256, 64, 256], P('fx', 'cable', 'fz'), may hold values from 0.02 to 0.15
- disp_init: float32 [3, 16384], P(None, ('cable', 'fx', 'fz')), may hold values from -3 to 3
- rest_shape: float32 [3, 16384], P(None, ('cable', 'fx', 'fz')), may hold values from -6 to 6
- compliance: float32 [16384], P(('cable', 'fx', 'fz')), may hold values from 0.5 to 2
- stencil_weights: float32 [3, 12, 16384], P(None, None, ('cable', 'fx', 'fz')), may hold values from 0.05 to 0.45
- anchor: int32 [3, 16384], P(None, ('cable', 'fx', 'fz')), may hold values from 0 to 9852, as said below
- owners: int32 [3, 16384], P(None, ('cable', 'fx', 'fz')), may hold values from 0 to 63, as said below
Outputs:
- disp_next: float32 [3, 16384], P(None, ('cable', 'fx', 'fz'))
- velocity_out: float32 [3, 256, 64, 256], P(None, 'fx', 'cable', 'fz')
Inputs may be any that keep to these rules, and one draw needn't show every extreme that they name: `owners`: the owner's number is fx * 2 + fz of a fluid block in the segment's own cable group. Among the 64 segments of one device (aligned blocks of 64 segments), at most 4 name the same owner in one iteration; in every iteration one owner is named by exactly 4 segments of every device of each group. `anchor`: the cell is numbered (x * 16 + y) * 128 + z in the owner's block, with x <= 4, y <= 12 and z <= 124, so the 4 x 4 x 4 stencil lies inside that block.
All inputs are finite; a program needn't handle non-finite values.
Results may differ from a plain program's by a relative error of at most 0.0003.
Values sent between devices are 32-bit elements; how exact they have to be, the bound alone decides.
No kernel may reach another device: no remote copies, remote signals or barrier semaphores. Data moves between devices by JAX's collectives and lax.ppermute only.
A program may use at most 64 MiB of HBM per device.

v0:
```python
import jax
import jax.numpy as jnp
from jax import lax
from jax.sharding import PartitionSpec as P

ITERS = 3
spread_gain = 16.0
drag_coeff = 0.05
relaxation = 0.5
ridge_share = 0.01


def with_halo(cells, sides, width):
    for axis, dim in sides:
        count = lax.axis_size(axis)
        ends = count - 1
        head = lax.slice_in_dim(cells, 0, width, axis=dim)
        tail = lax.slice_in_dim(cells, cells.shape[dim] - width, cells.shape[dim], axis=dim)
        cells = jnp.concatenate(
            [
                lax.ppermute(tail, axis, [(i, (i + 1) % count) for i in range(ends)]),
                cells,
                lax.ppermute(head, axis, [((i + 1) % count, i) for i in range(ends)]),
            ],
            axis=dim,
        )
    return cells


def stencil_table(weights):
    table = (
        weights[0:4][:, None, None, :]
        * weights[4:8][None, :, None, :]
        * weights[8:12][None, None, :, :]
    )
    return table.reshape(64, weights.shape[1])


def face_sum(padded):
    beside = padded[:, 2:, 1:-1, 1:-1] + padded[:, :-2, 1:-1, 1:-1]
    beside = beside + padded[:, 1:-1, 2:, 1:-1] + padded[:, 1:-1, :-2, 1:-1]
    beside = beside + padded[:, 1:-1, 1:-1, 2:] + padded[:, 1:-1, 1:-1, :-2]
    return beside


def solve_small(gram, width):
    square = gram[:width, :width]
    target = gram[:width, width]
    shift = ridge_share * jnp.trace(square) / width + 1e-06
    if width == 1:
        return [-target[0] / (square[0, 0] + shift)]
    first = square[0, 0] + shift
    second = square[1, 1] + shift
    cross = square[0, 1]
    determinant = first * second - cross * cross
    return [
        -(second * target[0] - cross * target[1]) / determinant,
        -(first * target[1] - cross * target[0]) / determinant,
    ]


def body(velocity, viscosity, disp_init, rest_shape, compliance, stencil_weights, anchor, owners):
    member = lax.axis_index(("fx", "fz"))
    seg_count = disp_init.shape[1]
    seg_total = seg_count * lax.axis_size(("cable", "fx", "fz"))
    position = lax.axis_index(("cable", "fx", "fz")) * seg_count + jnp.arange(
        seg_count, dtype=jnp.int32
    )
    tension_ramp = 1.0 + 2.0 * position.astype(jnp.float32) / seg_total
    size_x, size_y, size_z = viscosity.shape
    cells = size_x * size_y * size_z
    slot_total = 4 * seg_count
    steps_one = jnp.arange(4, dtype=jnp.int32)
    offsets = (
        (steps_one[:, None, None] * size_y + steps_one[None, :, None]) * size_z
        + steps_one[None, None, :]
    ).reshape(64)
    current = disp_init
    residuals = []
    responses = []
    velocity_out = velocity
    for iteration in range(ITERS):
        corner_row = anchor[iteration].astype(jnp.float32)[None]
        payload = jnp.concatenate([current, stencil_weights[iteration], corner_row], axis=0)
        owner_row = owners[iteration].astype(jnp.float32)[None]
        everyone = lax.all_gather(
            jnp.concatenate([payload, owner_row], axis=0), ("fx", "fz"), axis=1, tiled=True
        )
        owned = (everyone[16].astype(jnp.int32) == member).astype(jnp.int32)
        rank = jnp.cumsum(owned) - owned
        slot_place = jnp.where(owned > 0, rank, slot_total)
        compact = (
            jnp.zeros((16, slot_total + 1), jnp.float32)
            .at[:, slot_place]
            .set(everyone[0:16])[:, :slot_total]
        )
        corner = compact[15].astype(jnp.int32)
        cell_index = corner[None, :] + offsets[:, None]
        stencil = stencil_table(compact[3:15])
        spread_terms = spread_gain * stencil[None] * compact[0:3][:, None, :]
        forcing = (
            jnp.zeros((3, cells), jnp.float32)
            .at[:, cell_index.reshape(-1)]
            .add(spread_terms.reshape(3, -1))
        )
        forcing_field = forcing.reshape(velocity.shape)
        u_star = velocity + forcing_field
        padded = with_halo(u_star, (("cable", 2), ("fx", 1), ("fz", 3)), 1)
        beside = face_sum(padded)
        laplace = beside - 6.0 * u_star
        speed = jnp.sqrt(1.0 + jnp.sum(u_star * u_star, axis=0, keepdims=True))
        u_new = u_star + viscosity[None] * laplace - drag_coeff * u_star * speed
        picked = u_new.reshape(3, cells)[:, cell_index]
        sampled = jnp.sum(stencil[None] * picked, axis=1)
        widened = jnp.concatenate([sampled, jnp.zeros((3, 1), jnp.float32)], axis=1)
        spread_back = widened[:, slot_place]
        returned = lax.psum_scatter(spread_back, ("fx", "fz"), scatter_dimension=1, tiled=True)
        response = rest_shape + compliance[None] * tension_ramp[None] * returned
        response, velocity_out = (response, u_new)
        residual = response - current
        if iteration == 0:
            following = current + relaxation * residual
        else:
            columns = [residual - earlier for earlier in residuals]
            changes = [response - earlier for earlier in responses]
            matrix = jnp.stack(columns + [residual]).reshape(iteration + 1, -1)
            partial_gram = jnp.dot(matrix, matrix.T, precision=lax.Precision.HIGHEST)
            gram = lax.psum(partial_gram, ("cable", "fx", "fz"))
            coefs = solve_small(gram, iteration)
            following = response
            for column in range(iteration):
                following = following + coefs[column] * changes[column]
        residuals.append(residual)
        responses.append(response)
        current = following
    return (current, velocity_out)


def solution(mesh):
    placed = (
        P(None, "fx", "cable", "fz"),
        P("fx", "cable", "fz"),
        P(None, ("cable", "fx", "fz")),
        P(None, ("cable", "fx", "fz")),
        P(("cable", "fx", "fz")),
        P(None, None, ("cable", "fx", "fz")),
        P(None, ("cable", "fx", "fz")),
        P(None, ("cable", "fx", "fz")),
    )
    return jax.shard_map(
        body,
        mesh=mesh,
        in_specs=placed,
        out_specs=(P(None, ("cable", "fx", "fz")), P(None, "fx", "cable", "fz")),
        check_vma=False,
    )
```

profile of v0, /device:TPU:1, one launch (start us, length us, event | category | flops | bytes accessed | tf_op | source)
XLA Modules:
  0.0 1473.1 jit_solution(890402977995218385)
XLA Ops:
  9.5 55.1 %all-gather = f32[64,64,17]{1,2,0:T(8,128)S(1)} all-gather(f32[1,64,17]{1,2,0:T(8,128)S(1)} %maximum_bitcast_fusion), channel_id=1, replica_groups=mesh['cable'=4,'fx'=32,'fz'=2] {'fx','fz'}, dimensions={0}, use_global_device_ids=true | all-gather | bytes 282880 | tf_op jit(solution)/shard_map/all_gather | solution.py:86
  66.2 10.6 scatter_custom_fusion
  82.6 109.0 %scatter_custom_fusion.1 = f32[3,16384]{0,1:T(8,128)} fusion(s32[16384]{0:T(1024)S(1)} %bitcast.195, f32[3,16384]{0,1:T(8,128)} %bitcast_multiply_fusion.2, f32[]{:T(128)} %constant.30.clone.1), kind=kCustom, calls=%fused_computation.18 | custom fusion | flops 49152 | bytes 393220 | tf_op jit(solution)/shard_map/scatter-add | solution.py:104
  191.6 5.3 copy.63
  225.2 57.8 %gather_fusion = f32[16384,3]{1,0:T(8,128)} fusion(f32[3,16384]{0,1:T(8,128)} %bitcast.156, s32[16384]{0:T(1024)S(1)} %broadcast_clamp_fusion.2), kind=kCustom, calls=%fused_computation | custom fusion | bytes 458752 | tf_op jit(solution)/shard_map/gather | solution.py:113
  283.0 5.3 multiply_reduce_fusion.2
  288.3 14.1 gather_fusion.1
  302.5 137.5 %reduce-scatter.10.cloned.1.call-done = f32[64,3]{1,0:T(8,128)} async-done(((f32[4096,3]{1,0:T(8,128)}), f32[64,3]{1,0:T(8,128)}) %reduce-scatter.10.cloned.1.call-update) | async-done | bytes 784
  440.9 55.0 %all-gather.1 = f32[64,64,17]{1,2,0:T(8,128)S(1)} all-gather(f32[1,64,17]{1,2,0:T(8,128)S(1)} %maximum_bitcast_fusion.1), channel_id=1, replica_groups=mesh['cable'=4,'fx'=32,'fz'=2] {'fx','fz'}, dimensions={0}, use_global_device_ids=true | all-gather | bytes 282880 | tf_op jit(solution)/shard_map/all_gather | solution.py:86
  497.5 10.6 scatter_custom_fusion.2
  513.8 108.7 %scatter_custom_fusion.3 = f32[3,16384]{0,1:T(8,128)} fusion(s32[16384]{0:T(1024)S(1)} %bitcast.196, f32[3,16384]{0,1:T(8,128)} %bitcast_multiply_fusion.1, f32[]{:T(128)} %constant.30.clone.1), kind=kCustom, calls=%fused_computation.15 | custom fusion | flops 49152 | bytes 393220 | tf_op jit(solution)/shard_map/scatter-add | solution.py:104
  656.1 57.8 %gather_fusion.2 = f32[16384,3]{1,0:T(8,128)} fusion(f32[3,16384]{0,1:T(8,128)} %bitcast.157, s32[16384]{0:T(1024)S(1)} %broadcast_clamp_fusion.1), kind=kCustom, calls=%fused_computation.2 | custom fusion | bytes 458752 | tf_op jit(solution)/shard_map/gather | solution.py:113
  713.9 5.3 multiply_reduce_fusion.1
  719.2 14.1 gather_fusion.3
  733.3 137.5 %reduce-scatter.12.cloned.1.call-done = f32[64,3]{1,0:T(8,128)} async-done(((f32[4096,3]{1,0:T(8,128)}), f32[64,3]{1,0:T(8,128)}) %reduce-scatter.12.cloned.1.call-update) | async-done | bytes 784
  871.8 79.6 %psum.14 = f32[2,2]{1,0:T(2,128)S(1)} all-reduce(f32[2,2]{1,0:T(2,128)S(1)} %convolution_bitcast_fusion.1), channel_id=1, replica_groups=mesh['cable'=4,'fx'=32,'fz'=2] {'cable','fx','fz'}, use_global_device_ids=true, to_apply=%region_14.15 | all-reduce | flops 4 | bytes 32 | tf_op jit(solution)/shard_map/psum | solution.py:128
  954.0 50.5 %all-gather.2 = f32[64,64,17]{1,2,0:T(8,128)S(1)} all-gather(f32[1,64,17]{1,2,0:T(8,128)S(1)} %maximum_bitcast_fusion.2), channel_id=1, replica_groups=mesh['cable'=4,'fx'=32,'fz'=2] {'fx','fz'}, dimensions={0}, use_global_device_ids=true | all-gather | bytes 282880 | tf_op jit(solution)/shard_map/all_gather | solution.py:86
  1006.2 10.6 scatter_custom_fusion.4
  1022.4 109.0 %scatter_custom_fusion.5 = f32[3,16384]{0,1:T(8,128)} fusion(s32[16384]{0:T(1024)S(1)} %bitcast.197, f32[3,16384]{0,1:T(8,128)} %bitcast_multiply_fusion, f32[]{:T(128)} %constant.30.clone.1), kind=kCustom, calls=%fused_computation.12 | custom fusion | flops 49152 | bytes 393220 | tf_op jit(solution)/shard_map/scatter-add | solution.py:104
  1163.5 57.8 %gather_fusion.4 = f32[16384,3]{1,0:T(8,128)} fusion(f32[3,16384]{0,1:T(8,128)} %bitcast.158, s32[16384]{0:T(1024)S(1)} %broadcast_clamp_fusion), kind=kCustom, calls=%fused_computation.4 | custom fusion | bytes 458752 | tf_op jit(solution)/shard_map/gather | solution.py:113
  1221.2 5.2 multiply_reduce_fusion
  1226.5 14.1 gather_fusion.5
  1240.6 136.3 %reduce-scatter.14.cloned.1.call-done = f32[64,3]{1,0:T(8,128)} async-done(((f32[4096,3]{1,0:T(8,128)}), f32[64,3]{1,0:T(8,128)}) %reduce-scatter.14.cloned.1.call-update) | async-done | bytes 784
  1378.0 79.5 %psum.15 = f32[3,3]{1,0:T(4,128)S(1)} all-reduce(f32[3,3]{1,0:T(4,128)S(1)} %convolution_bitcast_fusion), channel_id=1, replica_groups=mesh['cable'=4,'fx'=32,'fz'=2] {'cable','fx','fz'}, use_global_device_ids=true, to_apply=%region_22.23 | all-reduce | flops 9 | bytes 72 | tf_op jit(solution)/shard_map/psum | solution.py:128
  (197 shorter events, 123.0 us)
Async XLA Ops:
  7.2 432.8 %reduce-scatter.10.cloned.1.call-start = ((), (), s32[]{:S(2)}) async-start(), calls=%async_computation.3 | async-start | bytes 2129920
  196.9 4.3 collective-permute-start
  199.7 4.7 collective-permute-start.1
  204.4 3.7 collective-permute-start.3
  206.8 4.7 collective-permute-start.2
  211.7 6.8 collective-permute-start.4
  216.7 3.6 collective-permute-start.5
  225.2 77.3 %copy-start.5 = (f32[64]{0:T(128)S(1)}, f32[64]{0:T(128)}, u32[]{:S(2)}) copy-start(f32[64]{0:T(128)} %param.12) | copy-start | bytes 772
  225.2 215.6 %copy-start.3 = (f32[3,64]{1,0:T(4,128)S(1)}, f32[3,64]{1,0:T(4,128)}, u32[]{:S(2)}) copy-start(f32[3,64]{1,0:T(4,128)} %param.11) | copy-start | bytes 2308
  225.2 215.6 %copy-start.4 = (f32[3,64]{1,0:T(4,128)S(1)}, f32[3,64]{1,0:T(4,128)}, u32[]{:S(2)}) copy-start(f32[3,64]{1,0:T(4,128)} %param.10) | copy-start | bytes 2308
  302.4 568.4 %reduce-scatter.12.cloned.1.call-start = ((), (), s32[]{:S(2)}) async-start(), calls=%async_computation.4 | async-start | bytes 2129920
  627.8 4.6 collective-permute-start.6
  631.1 4.4 collective-permute-start.7
  635.5 3.3 collective-permute-start.9
  637.5 4.7 collective-permute-start.8
  642.5 6.6 collective-permute-start.10
  647.6 3.6 collective-permute-start.11
  733.3 643.7 %reduce-scatter.14.cloned.1.call-start = ((), (), s32[]{:S(2)}) async-start(), calls=%async_computation.5 | async-start | bytes 2129920
  1136.7 2.6 collective-permute-start.12
  1138.0 4.4 collective-permute-start.13
  1142.5 3.9 collective-permute-start.15
  1145.0 4.7 collective-permute-start.14
  1150.0 6.3 collective-permute-start.16
  1154.9 3.6 collective-permute-start.17
  (3 other events, 101.6 us)
Sparse Core Ops, SparseCore 0:
  302.5 137.4 reduce-scatter.9
  733.4 137.3 reduce-scatter.11
  1240.8 136.1 reduce-scatter.13
where the time goes:
time: 1480 us; the launch traced here: 1470 us
  waiting for transfers between devices  437 us (30%)
  other arithmetic  363 us (25%)
  blocking collectives  320 us (22%)
  local copies, waits for them, and re-layouts  287 us (19%)
  starting transfers between devices  41.6 us (3%)
  between operations  23.9 us (2%)
    unnamed x6, waiting for transfers between devices  411 us
    scatter-add x3, other arithmetic, body(): forcing = jnp.zeros((3, cells), jnp.float32).at[:, cell_index.reshape(-1)...  327 us
    gather x3, local copies, waits for them, and re-layouts, body(): picked = u_new.reshape(3, cells)[:, cell_index]  173 us
    all_gather x3, blocking collectives, body(): lax.all_gather(jnp.concatenate([payload, owner_row], axis=0), ('fx', 'fz'...  161 us
    psum x2, blocking collectives, body(): gram = lax.psum(partial_gram, ('cable', 'fx', 'fz'))  159 us
    gather x3, local copies, waits for them, and re-layouts, body(): spread_back = widened[:, slot_place]  42.3 us
    scatter x3, local copies, waits for them, and re-layouts, body(): compact = jnp.zeros((16, slot_total + 1), jnp.float32).at[:, slot_place]....  31.9 us
  transfers between devices with their start and end apart: 21, of which 12 were waited for; matrix products, arithmetic and copies ran while one was open for 0% of the time, Pallas kernels for 0%

commit v1 on v0

--- a/solution.py
+++ b/solution.py
@@ -83,8 +83,16 @@
         corner_row = anchor[iteration].astype(jnp.float32)[None]
         payload = jnp.concatenate([current, stencil_weights[iteration], corner_row], axis=0)
         owner_row = owners[iteration].astype(jnp.float32)[None]
-        everyone = lax.all_gather(
-            jnp.concatenate([payload, owner_row], axis=0), ("fx", "fz"), axis=1, tiled=True
+        everyone = jnp.concatenate(
+            lax.all_to_all(
+                jnp.stack(
+                    [jnp.concatenate([payload, owner_row], axis=0)] * lax.axis_size(("fx", "fz"))
+                ),
+                ("fx", "fz"),
+                0,
+                0,
+            ),
+            axis=1,
         )
         owned = (everyone[16].astype(jnp.int32) == member).astype(jnp.int32)
         rank = jnp.cumsum(owned) - owned

time: 1480 us -> 1400 us (0.946)
  blocking collectives: 320 us -> 207 us
  starting transfers between devices: 41.6 us -> 56.6 us
    all_gather x3 -> x0, blocking collectives: 161 us -> none  [body(): lax.all_gather(jnp.concatenate([payload, owner_row], axis=0), ('fx', 'fz'...]
    all_to_all x0 -> x2, blocking collectives: none -> 47.4 us  [body(): lax.all_to_all(jnp.stack([jnp.concatenate([payload, owner_row], axis=0)]...]
  transfers between devices with their start and end apart: 21 -> 22, of which waited for: 12 -> 13; matrix products, arithmetic and copies ran while one was open for 0% -> 0% of each run, Pallas kernels for 0% -> 0%
where the time goes in v1:
time: 1400 us; the launch traced here: 1390 us
  waiting for transfers between devices  445 us (32%)
  other arithmetic  369 us (26%)
  local copies, waits for them, and re-layouts  292 us (21%)
  blocking collectives  207 us (15%)
  starting transfers between devices  56.6 us (4%)
  between operations  23.9 us (2%)
    unnamed x6, waiting for transfers between devices  406 us
    scatter-add x3, other arithmetic, body(): forcing = jnp.zeros((3, cells), jnp.float32).at[:, cell_index.reshape(-1)...  327 us
    gather x3, local copies, waits for them, and re-layouts, body(): picked = u_new.reshape(3, cells)[:, cell_index]  173 us
    psum x2, blocking collectives, body(): gram = lax.psum(partial_gram, ('cable', 'fx', 'fz'))  159 us
    all_to_all x2, blocking collectives, body(): lax.all_to_all(jnp.stack([jnp.concatenate([payload, owner_row], axis=0)]...  47.4 us
    gather x3, local copies, waits for them, and re-layouts, body(): spread_back = widened[:, slot_place]  42.3 us
    scatter x3, local copies, waits for them, and re-layouts, body(): compact = jnp.zeros((16, slot_total + 1), jnp.float32).at[:, slot_place]....  31.9 us
  transfers between devices with their start and end apart: 22, of which 13 were waited for; matrix products, arithmetic and copies ran while one was open for 0% of the time, Pallas kernels for 0%

profile of v1, /device:TPU:1, one launch (start us, length us, event | category | flops | bytes accessed | tf_op | source)
XLA Modules:
  0.0 1393.5 jit_solution(18408914018322801410)
XLA Ops:
  10.5 13.0 all-to-all-start
  23.8 13.4 all-to-all-done
  42.3 10.6 scatter_custom_fusion
  58.6 109.0 %scatter_custom_fusion.1 = f32[3,16384]{0,1:T(8,128)} fusion(s32[16384]{0:T(1024)S(1)} %bitcast.165, f32[3,16384]{0,1:T(8,128)} %bitcast_multiply_fusion.2, f32[]{:T(128)} %constant.30.clone.1), kind=kCustom, calls=%fused_computation.18 | custom fusion | flops 49152 | bytes 393220 | tf_op jit(solution)/shard_map/scatter-add | solution.py:112
  167.6 5.3 copy.84
  201.1 57.8 %gather_fusion = f32[16384,3]{1,0:T(8,128)} fusion(f32[3,16384]{0,1:T(8,128)} %bitcast.123, s32[16384]{0:T(1024)S(1)} %broadcast_clamp_fusion.2), kind=kCustom, calls=%fused_computation | custom fusion | bytes 458752 | tf_op jit(solution)/shard_map/gather | solution.py:121
  258.9 5.3 multiply_reduce_fusion.2
  264.2 14.1 %gather_fusion.1 = f32[4096,3]{1,0:T(8,128)} fusion(f32[3,257]{0,1:T(8,128)S(1)} %concatenate.102, s32[4096]{0:T(1024)S(1)} %broadcast_clamp_fusion.5), kind=kCustom, calls=%fused_computation.1 | custom fusion | bytes 114688 | tf_op jit(solution)/shard_map/gather | solution.py:124
  278.9 135.6 %reduce-scatter.10.cloned.1.call-done = f32[64,3]{1,0:T(8,128)} async-done(((f32[4096,3]{1,0:T(8,128)}), f32[64,3]{1,0:T(8,128)}) %reduce-scatter.10.cloned.1.call-update) | async-done | bytes 784
  415.8 26.3 %all_to_all.15 = f32[64,1,1088]{2,1,0:T(1,128)S(1)} all-to-all(f32[64,1,1088]{2,1,0:T(1,128)S(1)} %reshape.924), channel_id=1, replica_groups=mesh['cable'=4,'fx'=32,'fz'=2] {'fx','fz'}, dimensions={0} | all-to-all | bytes 557056 | tf_op jit(solution)/shard_map/all_to_all | solution.py:87
  446.2 10.6 scatter_custom_fusion.2
  462.4 108.7 %scatter_custom_fusion.3 = f32[3,16384]{0,1:T(8,128)} fusion(s32[16384]{0:T(1024)S(1)} %bitcast.166, f32[3,16384]{0,1:T(8,128)} %bitcast_multiply_fusion.1, f32[]{:T(128)} %constant.30.clone.1), kind=kCustom, calls=%fused_computation.15 | custom fusion | flops 49152 | bytes 393220 | tf_op jit(solution)/shard_map/scatter-add | solution.py:112
  591.9 5.3 collective-permute-start.10
  605.7 57.8 %gather_fusion.2 = f32[16384,3]{1,0:T(8,128)} fusion(f32[3,16384]{0,1:T(8,128)} %bitcast.124, s32[16384]{0:T(1024)S(1)} %broadcast_clamp_fusion.1), kind=kCustom, calls=%fused_computation.2 | custom fusion | bytes 458752 | tf_op jit(solution)/shard_map/gather | solution.py:121
  668.8 14.1 %gather_fusion.3 = f32[4096,3]{1,0:T(8,128)} fusion(f32[3,257]{0,1:T(8,128)S(1)} %concatenate.112, s32[4096]{0:T(1024)S(1)} %broadcast_clamp_fusion.4), kind=kCustom, calls=%fused_computation.3 | custom fusion | bytes 114688 | tf_op jit(solution)/shard_map/gather | solution.py:124
  683.0 135.3 %reduce-scatter.12.cloned.1.call-done = f32[64,3]{1,0:T(8,128)} async-done(((f32[4096,3]{1,0:T(8,128)}), f32[64,3]{1,0:T(8,128)}) %reduce-scatter.12.cloned.1.call-update) | async-done | bytes 784
  819.2 79.7 %psum.14 = f32[2,2]{1,0:T(2,128)S(1)} all-reduce(f32[2,2]{1,0:T(2,128)S(1)} %convolution_bitcast_fusion.1), channel_id=1, replica_groups=mesh['cable'=4,'fx'=32,'fz'=2] {'cable','fx','fz'}, use_global_device_ids=true, to_apply=%region_14.15 | all-reduce | flops 4 | bytes 32 | tf_op jit(solution)/shard_map/psum | solution.py:136
  901.9 21.1 %all_to_all.16 = f32[64,1,1088]{2,1,0:T(1,128)S(1)} all-to-all(f32[64,1,1088]{2,1,0:T(1,128)S(1)} %reshape.926), channel_id=1, replica_groups=mesh['cable'=4,'fx'=32,'fz'=2] {'fx','fz'}, dimensions={0} | all-to-all | bytes 557056 | tf_op jit(solution)/shard_map/all_to_all | solution.py:87
  927.1 10.6 scatter_custom_fusion.4
  943.4 109.0 %scatter_custom_fusion.5 = f32[3,16384]{0,1:T(8,128)} fusion(s32[16384]{0:T(1024)S(1)} %bitcast.167, f32[3,16384]{0,1:T(8,128)} %bitcast_multiply_fusion, f32[]{:T(128)} %constant.30.clone.1), kind=kCustom, calls=%fused_computation.12 | custom fusion | flops 49152 | bytes 393220 | tf_op jit(solution)/shard_map/scatter-add | solution.py:112
  1085.5 57.8 %gather_fusion.4 = f32[16384,3]{1,0:T(8,128)} fusion(f32[3,16384]{0,1:T(8,128)} %bitcast.125, s32[16384]{0:T(1024)S(1)} %broadcast_clamp_fusion), kind=kCustom, calls=%fused_computation.4 | custom fusion | bytes 458752 | tf_op jit(solution)/shard_map/gather | solution.py:121
  1148.6 14.1 %gather_fusion.5 = f32[4096,3]{1,0:T(8,128)} fusion(f32[3,257]{0,1:T(8,128)S(1)} %concatenate.122, s32[4096]{0:T(1024)S(1)} %broadcast_clamp_fusion.3), kind=kCustom, calls=%fused_computation.5 | custom fusion | bytes 114688 | tf_op jit(solution)/shard_map/gather | solution.py:124
  1162.7 134.6 %reduce-scatter.14.cloned.1.call-done = f32[64,3]{1,0:T(8,128)} async-done(((f32[4096,3]{1,0:T(8,128)}), f32[64,3]{1,0:T(8,128)}) %reduce-scatter.14.cloned.1.call-update) | async-done | bytes 784
  1298.3 79.6 %psum.15 = f32[3,3]{1,0:T(4,128)S(1)} all-reduce(f32[3,3]{1,0:T(4,128)S(1)} %convolution_bitcast_fusion), channel_id=1, replica_groups=mesh['cable'=4,'fx'=32,'fz'=2] {'cable','fx','fz'}, use_global_device_ids=true, to_apply=%region_22.23 | all-reduce | flops 9 | bytes 72 | tf_op jit(solution)/shard_map/psum | solution.py:136
  (218 shorter events, 141.1 us)
Async XLA Ops:
  10.5 26.7 %all-to-all-start = ((f32[64,1,1088]{2,1,0:T(1,128)}), f32[64,1,1088]{2,1,0:T(1,128)S(1)}, u32[]{:S(2)}, u32[]{:S(2)}) async-start(f32[64,1,1088]{2,1,0:T(1,128)} %reshape.922), calls=%async_computation | async-start | bytes 589824 | tf_op jit(solution)/shard_map/all_to_all | solution.py:87
  23.5 390.9 %reduce-scatter.10.cloned.1.call-start = ((), (), s32[]{:S(2)}) async-start(), calls=%async_computation.6 | async-start | bytes 2129920
  172.9 4.1 collective-permute-start
  175.7 4.7 collective-permute-start.1
  180.4 3.4 collective-permute-start.3
  182.5 4.7 collective-permute-start.2
  187.4 6.5 collective-permute-start.4
  192.6 3.6 collective-permute-start.5
  201.1 214.2 %copy-start.3 = (f32[3,64]{1,0:T(4,128)S(1)}, f32[3,64]{1,0:T(4,128)}, u32[]{:S(2)}) copy-start(f32[3,64]{1,0:T(4,128)} %param.11) | copy-start | bytes 2308
  201.1 214.2 %copy-start.4 = (f32[3,64]{1,0:T(4,128)S(1)}, f32[3,64]{1,0:T(4,128)}, u32[]{:S(2)}) copy-start(f32[3,64]{1,0:T(4,128)} %param.10) | copy-start | bytes 2308
  278.3 539.9 %reduce-scatter.12.cloned.1.call-start = ((), (), s32[]{:S(2)}) async-start(), calls=%async_computation.7 | async-start | bytes 2129920
  576.5 4.8 collective-permute-start.6
  579.9 4.4 collective-permute-start.7
  584.4 3.9 collective-permute-start.9
  587.0 4.7 collective-permute-start.8
  591.9 6.6 collective-permute-start.10
  597.2 3.6 collective-permute-start.11
  682.9 614.4 %reduce-scatter.14.cloned.1.call-start = ((), (), s32[]{:S(2)}) async-start(), calls=%async_computation.8 | async-start | bytes 2129920
  1057.7 3.7 collective-permute-start.12
  1060.1 4.4 collective-permute-start.13
  1064.6 3.6 collective-permute-start.15
  1066.9 4.7 collective-permute-start.14
  1071.8 6.7 collective-permute-start.16
  1077.0 3.6 collective-permute-start.17
  (4 other events, 179.3 us)
Sparse Core Ops, SparseCore 0:
  278.5 135.9 reduce-scatter.9
  683.0 135.1 reduce-scatter.11
  1162.8 134.4 reduce-scatter.13
